TPU v7x, 32 devices: a whole 2x2x4 slice. The times are simulated.
32 devices in a mesh: grp: 2 (over x), ctr: 16 (over z, y, core).
Axes of the slice: x: 2, y: 2, z: 4, core: 2. Of those that a mesh axis runs over, the one named last changes fastest.
Arguments:
- centres: bfloat16 [6144, 768], P(('grp', 'ctr')), parts along dimension 0
- sample_idx: int32 [1024], P(('grp', 'ctr')), parts along dimension 0, may hold values from 0 to 3071, as said below
- coef: float32 [6144], P(('grp', 'ctr')), parts along dimension 0
- metric_factor: bfloat16 [768, 768], replicated, may hold values from -0.21875 to 0.21875
Outputs:
- metric_new: float32 [1536, 768], P(('grp', 'ctr')), parts along dimension 0
- transformed: float32 [1024, 768], P(('grp', 'ctr')), parts along dimension 0
There are 2 independent parts, one for each index of `grp`. A program takes and returns all parts, laid end to end along the dimension named above; an argument that names none is the same for every part. Nothing has to cross between parts.
Inputs may be any that keep to these rules, and one draw needn't show every extreme that they name: The 32 samples of the k-th aligned block of sample_idx are distinct centres of the k-th block of 192 centres.
All inputs are finite; a program needn't handle non-finite values.
Results may differ from a plain program's by a relative error of at most 0.0031.
Values may be sent and summed in bfloat16 or wider, within the bound.
A program may use at most 128 MiB of HBM per device.

v0:
```python
import jax
import jax.numpy as jnp
from jax import lax
from jax.sharding import PartitionSpec as P


def block_grad(rows_u, v_own, sv_own, coef):
    width = rows_u.shape[1]
    su = jnp.sum(rows_u.astype(jnp.float32) ** 2, axis=1)
    cross = jnp.dot(rows_u, v_own.T, preferred_element_type=jnp.float32)
    dist_sq = jnp.maximum(su[:, None] + sv_own[None, :] - 2.0 * cross, 0.0)
    radius = jnp.sqrt(dist_sq / width + 1.0)
    weight = coef[None, :] * jnp.exp(-radius / 4.0) / (4.0 * width * radius)
    wround = weight.astype(jnp.bfloat16)
    return jnp.dot(wround, v_own, preferred_element_type=jnp.float32) - jnp.sum(weight, axis=1)[
        :, None
    ] * rows_u.astype(jnp.float32)


def local(centres, sample_idx, coef, metric_factor):
    width = centres.shape[1]
    own_count = sample_idx.shape[0]
    devices = lax.axis_size("ctr")
    offset = lax.axis_index("ctr") * centres.shape[0]
    own_rows = jnp.take(centres, sample_idx - offset, axis=0)
    u_own = jnp.dot(own_rows, metric_factor, preferred_element_type=jnp.float32).astype(
        jnp.bfloat16
    )
    v_own = jnp.dot(centres, metric_factor, preferred_element_type=jnp.float32).astype(jnp.bfloat16)
    factor = metric_factor.astype(jnp.float32)
    coef_full = lax.all_gather(coef, "ctr", axis=0, tiled=True)
    piece = lax.all_gather(v_own, "ctr", axis=0, tiled=True)
    sv_piece = jnp.sum(piece.astype(jnp.float32) ** 2, axis=1)
    summed = block_grad(u_own, piece, sv_piece, coef_full)
    grads = jnp.dot(summed, factor.T, precision=lax.Precision.HIGHEST)
    local_outer = jnp.dot(grads.T, grads, precision=lax.Precision.HIGHEST) / (own_count * devices)
    agop = lax.psum(local_outer, "ctr")
    metric_full = agop * width / jnp.trace(agop)
    row_count = width // devices
    metric_rows = lax.dynamic_slice_in_dim(
        metric_full, lax.axis_index("ctr") * row_count, row_count, 0
    )
    transformed = jnp.dot(grads, metric_full, precision=lax.Precision.HIGHEST)
    return (metric_rows, transformed)


def solution(mesh):
    placed = (P(("grp", "ctr"), None), P(("grp", "ctr")), P(("grp", "ctr")), P())
    return jax.shard_map(
        local,
        mesh=mesh,
        in_specs=placed,
        out_specs=(P(("grp", "ctr"), None), P(("grp", "ctr"), None)),
        check_vma=False,
    )
```

profile of v0, /device:TPU:0, one launch (start us, length us, event | category | flops | bytes accessed | tf_op | source)
XLA Modules:
  0.0 199.3 jit_solution(7842170020570275571)
XLA Ops:
  7.2 0.0 copy-start
  7.2 0.0 copy-start.4
  7.2 0.0 copy-start.3
  7.2 0.0 all-gather.2.cloned.1.call-start
  7.2 1.2 copy-done
  8.4 2.1 %convolution_convert_fusion = bf16[192,768]{1,0:T(8,128)(2,1)} fusion(bf16[192,768]{1,0:T(8,128)(2,1)} %param.4, bf16[768,768]{1,0:T(8,128)(2,1)S(1)} %copy-done), kind=kOutput, calls=%fused_computation.12 | convolution fusion | flops 226639872 | bytes 1769472 | tf_op jit(solution)/shard_map/dot_general | solution.py:29
  10.5 0.0 all-gather.2.cloned.1.call-update
  10.5 0.0 all-reduce.3.cloned.1.call-start
  10.6 0.7 compare_and_fusion
  11.3 1.7 gather_fusion
  12.9 0.0 copy-done.4
  12.9 0.6 dynamic-slice
  14.2 0.0 copy-done.3
  14.2 0.3 dynamic-update-slice
  14.5 64.2 %all-reduce = f32[3072]{0:T(1024)S(1)} all-reduce(f32[3072]{0:T(1024)S(1)} %dynamic-update-slice), channel_id=1, replica_groups=mesh['grp'=2,'ctr'=16] {'ctr'}, use_global_device_ids=true, to_apply=%add | all-reduce | flops 3072 | bytes 24576
  78.7 0.5 fusion.6
  79.1 0.0 all-gather.2.cloned.1.call-done
  79.2 0.0 copy-start.1
  79.2 3.5 %multiply_reduce_fusion = f32[3072]{0:T(1024)S(1)} fusion(bf16[3072,768]{1,0:T(8,128)(2,1)} %all-gather.2.cloned.1.call-done), kind=kLoop, calls=%fused_computation.1 | loop fusion | flops 7074816 | bytes 4730880 | tf_op jit(solution)/shard_map/reduce_sum | solution.py:33
  82.7 0.3 copy-done.1
  82.9 1.7 fusion.11
  84.6 0.9 convolution_subtract_fusion
  85.4 1.1 fusion.12
  86.6 3.5 %convolution_multiply_fusion.1 = f32[768,768]{1,0:T(8,128)} fusion(f32[32,768]{1,0:T(8,128)S(1)} %fusion.12), kind=kOutput, calls=%fused_computation.11 | convolution fusion | flops 227082240 | bytes 2457600 | tf_op jit(solution)/shard_map/dot_general | solution.py:36
  90.1 0.0 all-reduce.3.cloned.1.call-update
  90.1 96.2 %all-reduce.3.cloned.1.call-done = f32[768,768]{1,0:T(8,128)} async-done(((f32[768,768]{1,0:T(8,128)}), f32[768,768]{1,0:T(8,128)}) %all-reduce.3.cloned.1.call-update) | async-done | bytes 2359312 | tf_op jit(solution)/shard_map/psum | solution.py:37
  186.3 0.0 copy-start.2
  186.3 2.5 %select_reduce_fusion = f32[]{:T(128)} fusion(f32[768,768]{1,0:T(8,128)} %all-reduce.3.cloned.1.call-done), kind=kLoop, calls=%fused_computation.8 | loop fusion | flops 1769471 | bytes 2359300 | tf_op jit(solution)/shard_map/jit(trace)/reduce_sum | solution.py:38
  188.8 0.0 copy-done.2
  188.8 0.8 multiply_divide_fusion
  189.7 2.1 %fusion.13 = f32[32,768]{1,0:T(8,128)} fusion(f32[32,768]{1,0:T(8,128)S(1)} %fusion.12, f32[768,768]{1,0:T(8,128)S(1)} %multiply_divide_fusion), kind=kOutput, calls=%fused_computation.30 | convolution fusion | flops 226492416 | bytes 2555904 | tf_op jit(solution)/shard_map/dot_general | solution.py:43
  191.7 0.7 constant_dynamic-slice_fusion
  (2 shorter events, 0.0 us)
Async XLA Ops:
  7.2 1.3 copy-start
  7.2 5.8 %copy-start.4 = (u32[32]{0:T(128)S(1)}, u32[32]{0:T(128)}, u32[]{:S(2)}) copy-start(u32[32]{0:T(128)} %constant.52) | copy-start | bytes 388
  7.2 7.0 %copy-start.3 = (f32[192]{0:T(256)S(1)}, f32[192]{0:T(256)}, u32[]{:S(2)}) copy-start(f32[192]{0:T(256)} %param.6) | copy-start | bytes 2308
  7.2 72.0 %all-gather.2.cloned.1.call-start = ((), (), s32[]{:S(2)}) async-start(), calls=%async_computation | async-start | bytes 5013504 | tf_op jit(solution)/shard_map/all_gather | solution.py:32
  10.5 175.8 %all-reduce.3.cloned.1.call-start = ((), (), s32[]{:S(2)}) async-start(), calls=%async_computation.1 | async-start | bytes 4718592 | tf_op jit(solution)/shard_map/psum | solution.py:37
  79.2 3.8 %copy-start.1 = (bf16[3072,768]{1,0:T(8,128)(2,1)S(1)}, bf16[3072,768]{1,0:T(8,128)(2,1)}, u32[]{:S(2)}) copy-start(bf16[3072,768]{1,0:T(8,128)(2,1)} %all-gather.2.cloned.1.call-done) | copy-start | bytes 14155780
  186.3 2.5 %copy-start.2 = (f32[768,768]{1,0:T(8,128)S(1)}, f32[768,768]{1,0:T(8,128)}, u32[]{:S(2)}) copy-start(f32[768,768]{1,0:T(8,128)} %all-reduce.3.cloned.1.call-done) | copy-start | bytes 7077892
Sparse Core Ops, SparseCore 0:
  10.7 56.3 all-gather.1
  90.2 96.0 all-reduce.2
where the time goes:
time: 200 us; the launch traced here: 199 us
  waiting for transfers between devices  96.3 us (48%)
  blocking collectives  64.2 us (32%)
  between operations  14.8 us (7%)
  matrix products  11.8 us (6%)
  other arithmetic  7.48 us (4%)
  local copies, waits for them, and re-layouts  4.68 us (2%)
    psum x1, waiting for transfers between devices, local(): agop = lax.psum(local_outer, 'ctr')  96.2 us
    unnamed x1, blocking collectives  64.2 us
  transfers between devices with their start and end apart: 2, of which 1 were waited for; matrix products, arithmetic and copies ran while one was open for 2% of the time, Pallas kernels for 0%

commit v1 on v0

--- a/solution.py
+++ b/solution.py
@@ -34,7 +34,9 @@
     summed = block_grad(u_own, piece, sv_piece, coef_full)
     grads = jnp.dot(summed, factor.T, precision=lax.Precision.HIGHEST)
     local_outer = jnp.dot(grads.T, grads, precision=lax.Precision.HIGHEST) / (own_count * devices)
-    agop = lax.psum(local_outer, "ctr")
+    agop = local_outer
+    for hop in (1, 2, 4, 8):
+        agop = agop + lax.ppermute(agop, "ctr", [(dev, dev ^ hop) for dev in range(16)])
     metric_full = agop * width / jnp.trace(agop)
     row_count = width // devices
     metric_rows = lax.dynamic_slice_in_dim(

time: 200 us -> 318 us (1.59)
  waiting for transfers between devices: 96.3 us -> 213 us
    ppermute x0 -> x4, waiting for transfers between devices: none -> 213 us  [local(): lax.ppermute(agop, 'ctr', [(dev, dev ^ hop) for dev in range(16)])]
    psum x1 -> x0, waiting for transfers between devices: 96.2 us -> none  [local(): agop = lax.psum(local_outer, 'ctr')]
  transfers between devices with their start and end apart: 2 -> 5, of which waited for: 1 -> 4; matrix products, arithmetic and copies ran while one was open for 2% -> 1% of each run, Pallas kernels for 0% -> 0%
where the time goes in v1:
time: 318 us
  waiting for transfers between devices  213 us (67%)
  blocking collectives  64.2 us (20%)
  between operations  14.9 us (5%)
  matrix products  10.4 us (3%)
  other arithmetic  10 us (3%)
  local copies, waits for them, and re-layouts  4.68 us (1%)
    ppermute x4, waiting for transfers between devices, local(): lax.ppermute(agop, 'ctr', [(dev, dev ^ hop) for dev in range(16)])  213 us
    unnamed x1, blocking collectives  64.2 us
  transfers between devices with their start and end apart: 5, of which 4 were waited for; matrix products, arithmetic and copies ran while one was open for 1% of the time, Pallas kernels for 0%

profile of v1, /device:TPU:0, one launch (start us, length us, event | category | flops | bytes accessed | tf_op | source)
XLA Modules:
  0.0 317.8 jit_solution(11110390465922464809)
XLA Ops:
  7.2 0.0 all-gather.2.cloned.1.call-start
  7.2 1.2 copy-done
  8.4 2.1 convolution_convert_fusion
  10.5 0.0 all-gather.2.cloned.1.call-update
  10.6 0.7 compare_and_fusion
  11.2 1.7 gather_fusion
  12.9 0.6 dynamic-slice
  14.2 0.3 dynamic-update-slice
  14.4 64.2 %all-reduce = f32[3072]{0:T(1024)S(1)} all-reduce(f32[3072]{0:T(1024)S(1)} %dynamic-update-slice), channel_id=1, replica_groups=mesh['grp'=2,'ctr'=16] {'ctr'}, use_global_device_ids=true, to_apply=%add | all-reduce | flops 3072 | bytes 24576
  78.6 0.5 fusion.6
  79.1 0.0 all-gather.2.cloned.1.call-done
  79.1 3.5 %multiply_reduce_fusion = f32[3072]{0:T(1024)S(1)} fusion(bf16[3072,768]{1,0:T(8,128)(2,1)} %all-gather.2.cloned.1.call-done), kind=kLoop, calls=%fused_computation.1 | loop fusion | flops 7074816 | bytes 4730880 | tf_op jit(solution)/shard_map/reduce_sum | solution.py:33
  82.6 0.3 copy-done.1
  82.9 1.6 fusion.11
  84.5 0.9 convolution_subtract_fusion
  85.4 1.1 fusion.12
  86.5 2.1 convolution_multiply_fusion.1
  88.7 0.1 collective-permute-start
  88.8 4.5 %collective-permute-done = f32[768,768]{1,0:T(8,128)S(1)} collective-permute-done((f32[768,768]{1,0:T(8,128)S(1)}, f32[768,768]{1,0:T(8,128)S(1)}, u32[]{:S(2)}, u32[]{:S(2)}) %collective-permute-start) | collective-permute-done | bytes 2359328 | tf_op jit(solution)/shard_map/ppermute | solution.py:39
  93.3 0.3 add.49
  93.6 0.1 collective-permute-start.1
  93.6 53.3 %collective-permute-done.1 = f32[768,768]{1,0:T(8,128)S(1)} collective-permute-done((f32[768,768]{1,0:T(8,128)S(1)}, f32[768,768]{1,0:T(8,128)S(1)}, u32[]{:S(2)}, u32[]{:S(2)}) %collective-permute-start.1) | collective-permute-done | bytes 2359328 | tf_op jit(solution)/shard_map/ppermute | solution.py:39
  146.9 0.3 add.50
  147.2 0.1 collective-permute-start.2
  147.3 52.4 %collective-permute-done.2 = f32[768,768]{1,0:T(8,128)S(1)} collective-permute-done((f32[768,768]{1,0:T(8,128)S(1)}, f32[768,768]{1,0:T(8,128)S(1)}, u32[]{:S(2)}, u32[]{:S(2)}) %collective-permute-start.2) | collective-permute-done | bytes 2359328 | tf_op jit(solution)/shard_map/ppermute | solution.py:39
  199.7 0.3 add.51
  200.0 0.1 collective-permute-start.3
  200.1 103.1 %collective-permute-done.3 = f32[768,768]{1,0:T(8,128)} collective-permute-done((f32[768,768]{1,0:T(8,128)S(1)}, f32[768,768]{1,0:T(8,128)}, u32[]{:S(2)}, u32[]{:S(2)}) %collective-permute-start.3) | collective-permute-done | bytes 2359328 | tf_op jit(solution)/shard_map/ppermute | solution.py:39
  303.2 2.4 select_reduce_fusion
  305.6 2.6 multiply_divide_fusion
  308.2 2.1 fusion.13
  310.3 0.7 constant_dynamic-slice_fusion
  (12 shorter events, 0.0 us)
Async XLA Ops:
  7.2 1.3 copy-start
  7.2 5.7 %copy-start.5 = (u32[32]{0:T(128)S(1)}, u32[32]{0:T(128)}, u32[]{:S(2)}) copy-start(u32[32]{0:T(128)} %constant.52) | copy-start | bytes 388
  7.2 7.0 %copy-start.4 = (f32[192]{0:T(256)S(1)}, f32[192]{0:T(256)}, u32[]{:S(2)}) copy-start(f32[192]{0:T(256)} %param.6) | copy-start | bytes 2308
  7.2 71.9 %all-gather.2.cloned.1.call-start = ((), (), s32[]{:S(2)}) async-start(), calls=%async_computation | async-start | bytes 5013504 | tf_op jit(solution)/shard_map/all_gather | solution.py:32
  79.1 3.8 %copy-start.1 = (bf16[3072,768]{1,0:T(8,128)(2,1)S(1)}, bf16[3072,768]{1,0:T(8,128)(2,1)}, u32[]{:S(2)}) copy-start(bf16[3072,768]{1,0:T(8,128)(2,1)} %all-gather.2.cloned.1.call-done) | copy-start | bytes 14155780
  86.5 2.2 copy-start.2
  88.7 4.6 %collective-permute-start = (f32[768,768]{1,0:T(8,128)S(1)}, f32[768,768]{1,0:T(8,128)S(1)}, u32[]{:S(2)}, u32[]{:S(2)}) collective-permute-start(f32[768,768]{1,0:T(8,128)S(1)} %convolution_multiply_fusion.1), channel_id=1, source_target_pairs={{0,1},{1,0},{2,3},{3,2},{4,5},{5,4},{6,7},{7,6},{8,9},{9,8},{10,11... | collective-permute-start | bytes 7077896 | tf_op jit(solution)/shard_map/ppermute | solution.py:39
  93.6 53.4 %collective-permute-start.1 = (f32[768,768]{1,0:T(8,128)S(1)}, f32[768,768]{1,0:T(8,128)S(1)}, u32[]{:S(2)}, u32[]{:S(2)}) collective-permute-start(f32[768,768]{1,0:T(8,128)S(1)} %add.49), channel_id=1, source_target_pairs={{0,2},{1,3},{2,0},{3,1},{4,6},{5,7},{6,4},{7,5},{8,10},{9,11},{10,... | collective-permute-start | bytes 7077896 | tf_op jit(solution)/shard_map/ppermute | solution.py:39
  147.2 52.5 %collective-permute-start.2 = (f32[768,768]{1,0:T(8,128)S(1)}, f32[768,768]{1,0:T(8,128)S(1)}, u32[]{:S(2)}, u32[]{:S(2)}) collective-permute-start(f32[768,768]{1,0:T(8,128)S(1)} %add.50), channel_id=1, source_target_pairs={{0,4},{1,5},{2,6},{3,7},{4,0},{5,1},{6,2},{7,3},{8,12},{9,13},{10,... | collective-permute-start | bytes 7077896 | tf_op jit(solution)/shard_map/ppermute | solution.py:39
  200.0 103.2 %collective-permute-start.3 = (f32[768,768]{1,0:T(8,128)S(1)}, f32[768,768]{1,0:T(8,128)}, u32[]{:S(2)}, u32[]{:S(2)}) collective-permute-start(f32[768,768]{1,0:T(8,128)S(1)} %add.51), channel_id=1, source_target_pairs={{0,8},{1,9},{2,10},{3,11},{4,12},{5,13},{6,14},{7,15},{8,0},{9,1},... | collective-permute-start | bytes 7077896 | tf_op jit(solution)/shard_map/ppermute | solution.py:39
  305.6 2.6 copy-start.3
Sparse Core Ops, SparseCore 0:
  10.7 56.3 all-gather.1
